TPU v7x, 128 devices: a whole 4x4x4 slice. The times are simulated.
128 devices in a mesh: by: 8 (over z, core), bx: 16 (over x, y).
Axes of the slice: x: 4, y: 4, z: 4, core: 2. Of those that a mesh axis runs over, the one named last changes fastest.
Arguments:
- tracers: float32 [20, 512, 16, 2048], P(None, ('by', 'bx')), may hold values from 0 to 1
- vertical_speed: float32 [20, 512, 2048], P(None, ('by', 'bx')), may hold values from -0.4 to 0.4
- diffusivity: float32 [20, 512, 2048], P(None, ('by', 'bx')), may hold values from 0.02 to 2
- buoyancy_force: bfloat16 [20, 512, 2048], P(None, ('by', 'bx')), may hold values from -2.1 to 2.1
- wet_levels: int32 [512, 2048], P(('by', 'bx')), may hold values from 0 to 20
- surface_patch: int32 [512, 2048], P(('by', 'bx')), may hold values from 0 to 15
- prior_height: float32 [512, 2048], P(('by', 'bx')), may hold values from -5 to 5
- land_mask: int32 [512, 16, 128], P(('by', 'bx')), may hold values 0 or 1
- baroclinic_map: int32 [512], replicated, may hold values from 0 to 511, as said below
- barotropic_map: int32 [512], replicated, may hold values from 0 to 511, as said below
Outputs:
- new_tracers: float32 [20, 512, 16, 2048], P(None, ('by', 'bx'))
- surface_height: float32 [512, 16, 128], P(('by', 'bx'))
Inputs may be any that keep to these rules, and one draw needn't show every extreme that they name: baroclinic_map[s] is the geographic block held in baroclinic slot s, blocks numbered row by row with 64 to a block row; it lies in block row s // 64, and every block appears once. barotropic_map[s] is the geographic block held in barotropic slot s, blocks numbered row by row with 64 to a block row; it lies in block row s // 64, and every block appears once.
All inputs are finite; a program needn't handle non-finite values. No bound on the sum of `land_mask` on one device may be relied on, other than what follows from the above.
Results may differ from a plain program's by a relative error of at most 0.0003.
Values sent between devices are 32-bit elements; how exact they have to be, the bound alone decides.
A program may use at most 128 MiB of HBM per device.

v0:
```python
import jax
import jax.numpy as jnp
from jax import lax
from jax.sharding import PartitionSpec as P

ITERS = 6
RESTORE = 0.5
SURFACE = 0.1
FACE_SCALE = 2.0
PRECISE = lax.Precision.HIGHEST


def padded_2(block, sides, width):
    for axis, dim in sides:
        count = lax.axis_size(axis)
        forward = [(i, i + 1) for i in range(count - 1)]
        backward = [(target, source) for source, target in forward]
        low = lax.ppermute(
            lax.slice_in_dim(block, block.shape[dim] - width, None, axis=dim), axis, forward
        )
        high = lax.ppermute(lax.slice_in_dim(block, 0, width, axis=dim), axis, backward)
        block = jnp.concatenate([low, block, high], axis=dim)
    return block


def column_step(tracers, vertical_speed, diffusivity, wet_levels, surface_patch):
    depth_index = lax.broadcasted_iota(jnp.int32, vertical_speed.shape, 0)
    wet_level = (depth_index < wet_levels[None]).astype(jnp.float32)
    open_faces = (depth_index + 1 < wet_levels[None]).astype(jnp.float32)
    speed_open = (vertical_speed * open_faces)[:, :, None]
    shifted_up = jnp.concatenate([tracers[1:], jnp.zeros_like(tracers[:1])], axis=0)
    flux_below = jnp.maximum(speed_open, 0.0) * shifted_up + jnp.minimum(speed_open, 0.0) * tracers
    flux_above = jnp.concatenate([jnp.zeros_like(flux_below[:1]), flux_below[:-1]], axis=0)
    advected = wet_level[:, :, None] * (tracers + flux_below - flux_above)
    mixing = diffusivity * open_faces
    mixing_above = jnp.concatenate([jnp.zeros_like(mixing[:1]), mixing[:-1]], axis=0)
    surface_row = (depth_index == 0).astype(jnp.float32) * wet_level * RESTORE
    diagonal = 1.0 + mixing + mixing_above + surface_row
    tracer_ids = lax.broadcasted_iota(jnp.int32, (1, tracers.shape[2], 1), 1)
    targets = (surface_patch[:, None, :] == tracer_ids).astype(jnp.float32)
    right_side = advected + surface_row[:, :, None] * targets[None]

    def forward(carry, layer):
        ratio_prev, value_prev = carry
        lower_band, diag_now, upper_band, right_now = layer
        pivot_now = diag_now - lower_band * ratio_prev
        ratio_now = upper_band / pivot_now
        value_now = (right_now - lower_band[:, None] * value_prev) / pivot_now[:, None]
        return ((ratio_now, value_now), (ratio_now, value_now))

    start_carry = (
        jnp.zeros(mixing.shape[1:], jnp.float32),
        jnp.zeros(tracers.shape[1:], jnp.float32),
    )
    ignored, (ratios, values) = lax.scan(
        forward, start_carry, (-mixing_above, diagonal, -mixing, right_side)
    )

    def backward(following, layer):
        ratio_now, value_now = layer
        solved_now = value_now - ratio_now[:, None] * following
        return (solved_now, solved_now)

    ignored_too, solved = lax.scan(
        backward, jnp.zeros(tracers.shape[1:], jnp.float32), (ratios, values), reverse=True
    )
    return solved


def local(
    tracers,
    vertical_speed,
    diffusivity,
    buoyancy_force,
    wet_levels,
    surface_patch,
    prior_height,
    land_mask,
    baroclinic_map,
    barotropic_map,
):
    blocks = wet_levels.shape[0]
    block_rows = land_mask.shape[1]
    block_cols = land_mask.shape[2]
    levels = vertical_speed.shape[0]
    band_row = lax.axis_index("by")
    column = lax.axis_index("bx")
    band_width = blocks * lax.axis_size("bx")
    band_first_slot = band_row * band_width
    clinic_band = (
        lax.dynamic_slice_in_dim(baroclinic_map, band_first_slot, band_width) - band_first_slot
    )
    tropic_band = (
        lax.dynamic_slice_in_dim(barotropic_map, band_first_slot, band_width) - band_first_slot
    )
    my_columns = lax.dynamic_slice_in_dim(tropic_band, column * blocks, blocks)
    depth_index = lax.broadcasted_iota(jnp.int32, buoyancy_force.shape, 0)
    wet_level = (depth_index < wet_levels[None]).astype(jnp.float32)
    forcing = jnp.sum(wet_level * buoyancy_force.astype(jnp.float32), axis=0)
    payload = jnp.stack([forcing, wet_levels.astype(jnp.float32), prior_height], axis=0)
    selector = (clinic_band[None, :] == my_columns[:, None]).astype(jnp.float32)
    relaid = jnp.einsum(
        "jt,qtc->qjc",
        selector,
        lax.all_gather(payload, "bx", axis=1, tiled=True),
        precision=PRECISE,
    )
    new_tracers = column_step(tracers, vertical_speed, diffusivity, wet_levels, surface_patch)
    shape_flat = (blocks, block_rows, block_cols)
    ocean_mask = land_mask.astype(jnp.float32)
    depth_field = relaid[1].reshape(shape_flat)
    source = ocean_mask * relaid[0].reshape(shape_flat)
    first_guess = ocean_mask * relaid[2].reshape(shape_flat)
    west_pick = (tropic_band[None, :] == (my_columns[:, None] - 1) % band_width).astype(jnp.float32)
    east_pick = (tropic_band[None, :] == (my_columns[:, None] + 1) % band_width).astype(jnp.float32)
    band_slots = lax.broadcasted_iota(jnp.int32, (band_width, 1), 0)
    geo_pick = (tropic_band[None, :] == band_slots).astype(jnp.float32)
    my_pick = (band_slots[:, 0][None, :] == my_columns[:, None]).astype(jnp.float32)

    def extend(field_blocks):
        edge_cols = jnp.stack([field_blocks[..., 0], field_blocks[..., -1]], axis=2)
        edge_rows = jnp.stack([field_blocks[..., 0, :], field_blocks[..., -1, :]], axis=2)
        gathered_cols, gathered_rows = (
            lax.all_gather(edge_cols, "bx", axis=1, tiled=True),
            lax.all_gather(edge_rows, "bx", axis=1, tiled=True),
        )
        geo_rows = jnp.einsum("ct,qtsw->sqcw", geo_pick, gathered_rows, precision=PRECISE)
        beside = padded_2(geo_rows, (("by", 0),), 1)
        north_side = jnp.einsum("jc,qcw->qjw", my_pick, beside[0], precision=PRECISE)
        south_side = jnp.einsum("jc,qcw->qjw", my_pick, beside[3], precision=PRECISE)
        west_side = jnp.einsum("jt,qth->qjh", west_pick, gathered_cols[:, :, 1], precision=PRECISE)
        east_side = jnp.einsum("jt,qth->qjh", east_pick, gathered_cols[:, :, 0], precision=PRECISE)
        middle = jnp.concatenate([west_side[..., None], field_blocks, east_side[..., None]], axis=3)
        north_row = jnp.pad(north_side, ((0, 0), (0, 0), (1, 1)))[:, :, None, :]
        south_row = jnp.pad(south_side, ((0, 0), (0, 0), (1, 1)))[:, :, None, :]
        return jnp.concatenate([north_row, middle, south_row], axis=2)

    statics = extend(jnp.stack([depth_field, ocean_mask], axis=0))
    depth_padded = statics[0]
    ocean_padded = statics[1]
    face_factor = FACE_SCALE / levels

    def face_weight(depth_other, ocean_other):
        return face_factor * jnp.minimum(depth_field, depth_other) * ocean_mask * ocean_other

    east_face = face_weight(depth_padded[:, 1:-1, 2:], ocean_padded[:, 1:-1, 2:])
    west_face = face_weight(depth_padded[:, 1:-1, :-2], ocean_padded[:, 1:-1, :-2])
    south_face = face_weight(depth_padded[:, 2:, 1:-1], ocean_padded[:, 2:, 1:-1])
    north_face = face_weight(depth_padded[:, :-2, 1:-1], ocean_padded[:, :-2, 1:-1])
    centre_weight = SURFACE * ocean_mask + (1.0 - ocean_mask)
    precond_diagonal = centre_weight + east_face + west_face + south_face + north_face

    def operate(field_blocks):
        padded = extend(field_blocks[None])[0]
        centre = centre_weight * field_blocks
        result = centre + east_face * (field_blocks - padded[:, 1:-1, 2:])
        result = result + west_face * (field_blocks - padded[:, 1:-1, :-2])
        result = result + south_face * (field_blocks - padded[:, 2:, 1:-1])
        return result + north_face * (field_blocks - padded[:, :-2, 1:-1])

    solution = first_guess
    residual = source - operate(solution)
    precond = residual / precond_diagonal

    def weighted(residual_now, precond_now):
        return lax.psum(jnp.sum(residual_now * precond_now), ("by", "bx"))

    direction = precond
    norm_now = weighted(residual, precond)
    for step_index in range(ITERS):
        image_field = operate(direction)
        step_size = norm_now / lax.psum(jnp.sum(direction * image_field), ("by", "bx"))
        solution = solution + step_size * direction
        residual = residual - step_size * image_field
        if step_index + 1 < ITERS:
            precond = residual / precond_diagonal
            norm_next = weighted(residual, precond)
            direction = precond + norm_next / norm_now * direction
            norm_now = norm_next
    return (new_tracers, solution)


def solution(mesh):
    return jax.shard_map(
        local,
        mesh=mesh,
        in_specs=(
            P(None, ("by", "bx"), None, None),
            P(None, ("by", "bx"), None),
            P(None, ("by", "bx"), None),
            P(None, ("by", "bx"), None),
            P(("by", "bx"), None),
            P(("by", "bx"), None),
            P(("by", "bx"), None),
            P(("by", "bx"), None, None),
            P(),
            P(),
        ),
        out_specs=(P(None, ("by", "bx"), None, None), P(("by", "bx"), None, None)),
        check_vma=False,
    )
```

profile of v0, /device:TPU:1, one launch (start us, length us, event | category | flops | bytes accessed | tf_op | source)
XLA Modules:
  0.0 1332.6 jit_solution(10514332008034676761)
XLA Ops:
  16.1 3.8 slice-done
  19.9 9.8 multiply_add_fusion.1
  29.7 9.2 slice.433
  38.9 15.5 %multiply_add_fusion = f32[20,4,16,2048]{3,2,1,0:T(8,128)} fusion(f32[19,4,16,2048]{3,2,1,0:T(8,128)} %slice.433, f32[20,4,16,2048]{3,2,1,0:T(8,128)} %param.14, f32[20,4,16,2048]{3,2,1,0:T(8,128)} %multiply_add_fusion.1, f32[4,16,2048]{2,1,0:T(8,128)S(1)} %fusion.3, f32[20,4,2048]{2,1,0:T(4,128)S(1)} %get-tuple-element.335, f32[20,4,2048]{2,1,0:T(4,128)S(1)} %fusion.2), kind=kLoop, calls=%fused_computation.13 | loop fusion | flops 13107200 | bytes 43253760 | tf_op jit(solution)/shard_map/add | solution.py:41
  54.4 5.3 broadcast.122.clone
  59.9 58.2 %while.34 = (s32[]{:T(128)}, f32[4,2048]{1,0:T(4,128)S(1)}, f32[4,16,2048]{2,1,0:T(8,128)S(1)}, f32[20,4,2048]{2,1,0:T(4,128)S(1)}, f32[20,4,16,2048]{3,2,1,0:T(...) while((s32[]{:T(128)}, f32[4,2048]{1,0:T(4,128)S(1)}, ...), condition=%wide.region_1.2_spmd.clone, body=%wide.region_0.0_spmd.clone.sunk | while | flops 557059 | bytes 2425468 | solution.py:55
  119.7 3.0 convolution_bitcast_fusion
  123.1 19.4 %all_gather.55 = f32[1,64,2,16]{3,2,0,1:T(2,128)S(1)} all-gather(f32[1,4,2,16]{3,2,0,1:T(2,128)S(1)} %copy.201), channel_id=1, replica_groups=mesh['by'=8,'bx'=16] {'bx'}, dimensions={1}, use_global_device_ids=true | all-gather | bytes 8704 | tf_op jit(solution)/shard_map/all_gather | solution.py:124
  142.9 17.5 %all_gather.54 = f32[1,64,2,128]{3,2,0,1:T(2,128)S(1)} all-gather(f32[1,4,2,128]{3,2,0,1:T(2,128)S(1)} %maximum_bitcast_fusion.7), channel_id=1, replica_groups=mesh['by'=8,'bx'=16] {'bx'}, dimensions={1}, use_global_device_ids=true | all-gather | bytes 69632 | tf_op jit(solution)/shard_map/all_gather | solution.py:125
  160.6 14.6 %collective-permute-start.2 = (f32[1,1,64,128]{3,2,0,1:T(8,128)S(1)}, f32[1,1,64,128]{3,2,0,1:T(8,128)S(1)}, u32[]{:S(2)}, u32[]{:S(2)}) collective-permute-start(f32[1,1,64,128]{3,2,0,1:T(8,128)S(1)} %get-tuple-element.331), channel_id=1, source_target_pairs={{0,16},{16,32},{32,48},{48,64},{64,80},{80,96},{96,112},{1,17},{17... | collective-permute-start | bytes 98312 | tf_op jit(solution)/shard_map/ppermute | solution.py:18
  177.4 16.0 %all_gather.53 = f32[2,64,2,16]{3,2,0,1:T(2,128)S(1)} all-gather(f32[2,4,2,16]{3,2,0,1:T(2,128)S(1)} %copy.191), channel_id=1, replica_groups=mesh['by'=8,'bx'=16] {'bx'}, dimensions={1}, use_global_device_ids=true | all-gather | bytes 17408 | tf_op jit(solution)/shard_map/all_gather | solution.py:124
  193.9 17.6 %all_gather.52 = f32[2,64,2,128]{3,2,0,1:T(2,128)S(1)} all-gather(f32[2,4,2,128]{3,2,0,1:T(2,128)S(1)} %fusion.130), channel_id=1, replica_groups=mesh['by'=8,'bx'=16] {'bx'}, dimensions={1}, use_global_device_ids=true | all-gather | bytes 139264 | tf_op jit(solution)/shard_map/all_gather | solution.py:125
  212.5 14.6 %collective-permute-start = (f32[1,2,64,128]{3,2,0,1:T(8,128)S(1)}, f32[1,2,64,128]{3,2,0,1:T(8,128)S(1)}, u32[]{:S(2)}, u32[]{:S(2)}) collective-permute-start(f32[1,2,64,128]{3,2,0,1:T(8,128)S(1)} %get-tuple-element.298), channel_id=1, source_target_pairs={{0,16},{16,32},{32,48},{48,64},{64,80},{80,96},{96,112},{1,17},{17... | collective-permute-start | bytes 196616 | tf_op jit(solution)/shard_map/ppermute | solution.py:18
  233.5 16.3 %all_gather.57 = f32[1,64,2,16]{3,2,0,1:T(2,128)S(1)} all-gather(f32[1,4,2,16]{3,2,0,1:T(2,128)S(1)} %copy.208), channel_id=1, replica_groups=mesh['by'=8,'bx'=16] {'bx'}, dimensions={1}, use_global_device_ids=true | all-gather | bytes 8704 | tf_op jit(solution)/shard_map/all_gather | solution.py:124
  250.1 17.4 %all_gather.56 = f32[1,64,2,128]{3,2,0,1:T(2,128)S(1)} all-gather(f32[1,4,2,128]{3,2,0,1:T(2,128)S(1)} %maximum_bitcast_fusion.8), channel_id=1, replica_groups=mesh['by'=8,'bx'=16] {'bx'}, dimensions={1}, use_global_device_ids=true | all-gather | bytes 69632 | tf_op jit(solution)/shard_map/all_gather | solution.py:125
  267.7 12.9 collective-permute-start.4
  283.2 3.0 collective-permute-done.5
  287.4 63.4 %all-reduce.19 = (f32[]{:T(128)}, f32[]{:T(128)}) all-reduce(f32[]{:T(128)} %get-tuple-element.217, f32[]{:T(128)} %get-tuple-element.216), channel_id=1, replica_groups=mesh['by'=8,'bx'=16] {'by','bx'}, use_global_device_ids=true, to_apply=%region_6.7 | all-reduce | flops 2 | bytes 16 | tf_op jit(solution)/shard_map/psum | solution.py:166
  352.7 63.8 %psum.86 = f32[]{:T(128)} all-reduce(f32[]{:T(128)} %get-tuple-element.276), channel_id=1, replica_groups=mesh['by'=8,'bx'=16] {'by','bx'}, use_global_device_ids=true, to_apply=%region_10.11 | all-reduce | flops 1 | bytes 8 | tf_op jit(solution)/shard_map/psum | solution.py:166
  418.1 16.0 %all_gather.59 = f32[1,64,2,16]{3,2,0,1:T(2,128)S(1)} all-gather(f32[1,4,2,16]{3,2,0,1:T(2,128)S(1)} %copy.215), channel_id=1, replica_groups=mesh['by'=8,'bx'=16] {'bx'}, dimensions={1}, use_global_device_ids=true | all-gather | bytes 8704 | tf_op jit(solution)/shard_map/all_gather | solution.py:124
  434.3 17.6 %all_gather.58 = f32[1,64,2,128]{3,2,0,1:T(2,128)S(1)} all-gather(f32[1,4,2,128]{3,2,0,1:T(2,128)S(1)} %maximum_bitcast_fusion.9), channel_id=1, replica_groups=mesh['by'=8,'bx'=16] {'bx'}, dimensions={1}, use_global_device_ids=true | all-gather | bytes 69632 | tf_op jit(solution)/shard_map/all_gather | solution.py:125
  452.1 13.6 %collective-permute-start.6 = (f32[1,1,64,128]{3,2,0,1:T(8,128)S(1)}, f32[1,1,64,128]{3,2,0,1:T(8,128)S(1)}, u32[]{:S(2)}, u32[]{:S(2)}) collective-permute-start(f32[1,1,64,128]{3,2,0,1:T(8,128)S(1)} %get-tuple-element.321), channel_id=1, source_target_pairs={{0,16},{16,32},{32,48},{48,64},{64,80},{80,96},{96,112},{1,17},{17... | collective-permute-start | bytes 98312 | tf_op jit(solution)/shard_map/ppermute | solution.py:18
  468.2 3.0 collective-permute-done.7
  472.4 63.4 %psum.87 = f32[]{:T(128)} all-reduce(f32[]{:T(128)} %get-tuple-element.274), channel_id=1, replica_groups=mesh['by'=8,'bx'=16] {'by','bx'}, use_global_device_ids=true, to_apply=%region_12.13 | all-reduce | flops 1 | bytes 8 | tf_op jit(solution)/shard_map/psum | solution.py:172
  537.7 62.6 %psum.88 = f32[]{:T(128)} all-reduce(f32[]{:T(128)} %get-tuple-element.271), channel_id=1, replica_groups=mesh['by'=8,'bx'=16] {'by','bx'}, use_global_device_ids=true, to_apply=%region_14.15 | all-reduce | flops 1 | bytes 8 | tf_op jit(solution)/shard_map/psum | solution.py:166
  601.9 17.5 %all_gather.61 = f32[1,64,2,16]{3,2,0,1:T(2,128)S(1)} all-gather(f32[1,4,2,16]{3,2,0,1:T(2,128)S(1)} %copy.222), channel_id=1, replica_groups=mesh['by'=8,'bx'=16] {'bx'}, dimensions={1}, use_global_device_ids=true | all-gather | bytes 8704 | tf_op jit(solution)/shard_map/all_gather | solution.py:124
  619.7 16.0 %all_gather.60 = f32[1,64,2,128]{3,2,0,1:T(2,128)S(1)} all-gather(f32[1,4,2,128]{3,2,0,1:T(2,128)S(1)} %maximum_bitcast_fusion.10), channel_id=1, replica_groups=mesh['by'=8,'bx'=16] {'bx'}, dimensions={1}, use_global_device_ids=true | all-gather | bytes 69632 | tf_op jit(solution)/shard_map/all_gather | solution.py:125
  635.9 15.2 %collective-permute-start.8 = (f32[1,1,64,128]{3,2,0,1:T(8,128)S(1)}, f32[1,1,64,128]{3,2,0,1:T(8,128)S(1)}, u32[]{:S(2)}, u32[]{:S(2)}) collective-permute-start(f32[1,1,64,128]{3,2,0,1:T(8,128)S(1)} %get-tuple-element.317), channel_id=1, source_target_pairs={{0,16},{16,32},{32,48},{48,64},{64,80},{80,96},{96,112},{1,17},{17... | collective-permute-start | bytes 98312 | tf_op jit(solution)/shard_map/ppermute | solution.py:18
  653.7 3.0 collective-permute-done.9
  657.8 62.1 %psum.89 = f32[]{:T(128)} all-reduce(f32[]{:T(128)} %get-tuple-element.269), channel_id=1, replica_groups=mesh['by'=8,'bx'=16] {'by','bx'}, use_global_device_ids=true, to_apply=%region_16.17 | all-reduce | flops 1 | bytes 8 | tf_op jit(solution)/shard_map/psum | solution.py:172
  721.9 64.2 %psum.90 = f32[]{:T(128)} all-reduce(f32[]{:T(128)} %get-tuple-element.266), channel_id=1, replica_groups=mesh['by'=8,'bx'=16] {'by','bx'}, use_global_device_ids=true, to_apply=%region_18.19 | all-reduce | flops 1 | bytes 8 | tf_op jit(solution)/shard_map/psum | solution.py:166
  787.6 16.1 %all_gather.63 = f32[1,64,2,16]{3,2,0,1:T(2,128)S(1)} all-gather(f32[1,4,2,16]{3,2,0,1:T(2,128)S(1)} %copy.229), channel_id=1, replica_groups=mesh['by'=8,'bx'=16] {'bx'}, dimensions={1}, use_global_device_ids=true | all-gather | bytes 8704 | tf_op jit(solution)/shard_map/all_gather | solution.py:124
  804.0 17.5 %all_gather.62 = f32[1,64,2,128]{3,2,0,1:T(2,128)S(1)} all-gather(f32[1,4,2,128]{3,2,0,1:T(2,128)S(1)} %maximum_bitcast_fusion.11), channel_id=1, replica_groups=mesh['by'=8,'bx'=16] {'bx'}, dimensions={1}, use_global_device_ids=true | all-gather | bytes 69632 | tf_op jit(solution)/shard_map/all_gather | solution.py:125
  821.6 12.6 collective-permute-start.10
  841.0 64.5 %psum.91 = f32[]{:T(128)} all-reduce(f32[]{:T(128)} %get-tuple-element.264), channel_id=1, replica_groups=mesh['by'=8,'bx'=16] {'by','bx'}, use_global_device_ids=true, to_apply=%region_20.21 | all-reduce | flops 1 | bytes 8 | tf_op jit(solution)/shard_map/psum | solution.py:172
  907.5 62.5 %psum.92 = f32[]{:T(128)} all-reduce(f32[]{:T(128)} %get-tuple-element.261), channel_id=1, replica_groups=mesh['by'=8,'bx'=16] {'by','bx'}, use_global_device_ids=true, to_apply=%region_22.23 | all-reduce | flops 1 | bytes 8 | tf_op jit(solution)/shard_map/psum | solution.py:166
  971.5 17.6 %all_gather.65 = f32[1,64,2,16]{3,2,0,1:T(2,128)S(1)} all-gather(f32[1,4,2,16]{3,2,0,1:T(2,128)S(1)} %copy.236), channel_id=1, replica_groups=mesh['by'=8,'bx'=16] {'bx'}, dimensions={1}, use_global_device_ids=true | all-gather | bytes 8704 | tf_op jit(solution)/shard_map/all_gather | solution.py:124
  989.4 16.0 %all_gather.64 = f32[1,64,2,128]{3,2,0,1:T(2,128)S(1)} all-gather(f32[1,4,2,128]{3,2,0,1:T(2,128)S(1)} %maximum_bitcast_fusion.12), channel_id=1, replica_groups=mesh['by'=8,'bx'=16] {'bx'}, dimensions={1}, use_global_device_ids=true | all-gather | bytes 69632 | tf_op jit(solution)/shard_map/all_gather | solution.py:125
  1005.6 15.0 %collective-permute-start.12 = (f32[1,1,64,128]{3,2,0,1:T(8,128)S(1)}, f32[1,1,64,128]{3,2,0,1:T(8,128)S(1)}, u32[]{:S(2)}, u32[]{:S(2)}) collective-permute-start(f32[1,1,64,128]{3,2,0,1:T(8,128)S(1)} %get-tuple-element.309), channel_id=1, source_target_pairs={{0,16},{16,32},{32,48},{48,64},{64,80},{80,96},{96,112},{1,17},{17... | collective-permute-start | bytes 98312 | tf_op jit(solution)/shard_map/ppermute | solution.py:18
  1023.2 3.0 collective-permute-done.13
  1027.3 62.1 %psum.93 = f32[]{:T(128)} all-reduce(f32[]{:T(128)} %get-tuple-element.259), channel_id=1, replica_groups=mesh['by'=8,'bx'=16] {'by','bx'}, use_global_device_ids=true, to_apply=%region_24.25 | all-reduce | flops 1 | bytes 8 | tf_op jit(solution)/shard_map/psum | solution.py:172
  1091.5 64.2 %psum.94 = f32[]{:T(128)} all-reduce(f32[]{:T(128)} %multiply_reduce_fusion), channel_id=1, replica_groups=mesh['by'=8,'bx'=16] {'by','bx'}, use_global_device_ids=true, to_apply=%region_26.27 | all-reduce | flops 1 | bytes 8 | tf_op jit(solution)/shard_map/psum | solution.py:166
  1157.2 16.1 %all_gather.67 = f32[1,64,2,16]{3,2,0,1:T(2,128)S(1)} all-gather(f32[1,4,2,16]{3,2,0,1:T(2,128)S(1)} %copy.243), channel_id=1, replica_groups=mesh['by'=8,'bx'=16] {'bx'}, dimensions={1}, use_global_device_ids=true | all-gather | bytes 8704 | tf_op jit(solution)/shard_map/all_gather | solution.py:124
  1173.6 17.5 %all_gather.66 = f32[1,64,2,128]{3,2,0,1:T(2,128)S(1)} all-gather(f32[1,4,2,128]{3,2,0,1:T(2,128)S(1)} %maximum_bitcast_fusion.13), channel_id=1, replica_groups=mesh['by'=8,'bx'=16] {'bx'}, dimensions={1}, use_global_device_ids=true | all-gather | bytes 69632 | tf_op jit(solution)/shard_map/all_gather | solution.py:125
  1191.3 12.6 collective-permute-start.14
  1210.7 5.4 broadcast.122
  1216.1 43.3 %while.35 = (s32[]{:T(128)}, f32[4,16,2048]{2,1,0:T(8,128)S(1)}, f32[20,4,16,2048]{3,2,1,0:T(8,128)}, f32[20,4,16,2048]{3,2,1,0:T(8,128)}, f32[20,4,2048]{2,1,0:T(4,128)S(1)}, /*index=5*/s32[]{:T(128)}, s32[]{:T(128)}, s32[]{:T(128)}) while((s32[]{:T(128)}, f32[4,16,2048]{2,1,0:T(8,128)S(1)}, f32[20,4,16,2048]{3,2,1,0:T(8,128)}, ...), condition=%wide.region_3.4_spmd.clone, body=%wide.region_2.3_spmd.clone.sunk | while | flops 393220 | bytes 2195571 | solution.py:64
  1259.4 64.3 %psum.95 = f32[]{:T(128)} all-reduce(f32[]{:T(128)} %fusion.39), channel_id=1, replica_groups=mesh['by'=8,'bx'=16] {'by','bx'}, use_global_device_ids=true, to_apply=%region_28.29 | all-reduce | flops 1 | bytes 8 | tf_op jit(solution)/shard_map/psum | solution.py:172
  (306 shorter events, 158.1 us)
Async XLA Ops:
  7.2 112.6 %all-gather.2.cloned.1.call-start = ((), (), s32[]{:S(2)}) async-start(), calls=%async_computation | async-start | bytes 2228224 | tf_op jit(solution)/shard_map/all_gather | solution.py:105
  16.1 3.8 slice-start
  29.7 9.2 copy-start.1
  54.4 65.2 %copy-start = (s32[4,16,128]{2,1,0:T(8,128)S(1)}, s32[4,16,128]{2,1,0:T(8,128)}, u32[]{:S(2)}) copy-start(s32[4,16,128]{2,1,0:T(8,128)} %param.21) | copy-start | bytes 98308
  160.6 68.4 %collective-permute-start.2 = (f32[1,1,64,128]{3,2,0,1:T(8,128)S(1)}, f32[1,1,64,128]{3,2,0,1:T(8,128)S(1)}, u32[]{:S(2)}, u32[]{:S(2)}) collective-permute-start(f32[1,1,64,128]{3,2,0,1:T(8,128)S(1)} %get-tuple-element.331), channel_id=1, source_target_pairs={{0,16},{16,32},{32,48},{48,64},{64,80},{80,96},{96,112},{1,17},{17... | collective-permute-start | bytes 98312 | tf_op jit(solution)/shard_map/ppermute | solution.py:18
  175.2 54.1 %collective-permute-start.3 = (f32[1,1,64,128]{3,2,0,1:T(8,128)S(1)}, f32[1,1,64,128]{3,2,0,1:T(8,128)S(1)}, u32[]{:S(2)}, u32[]{:S(2)}) collective-permute-start(f32[1,1,64,128]{3,2,0,1:T(8,128)S(1)} %get-tuple-element.332), channel_id=1, source_target_pairs={{16,0},{32,16},{48,32},{64,48},{80,64},{96,80},{112,96},{17,1},{33... | collective-permute-start | bytes 98312 | tf_op jit(solution)/shard_map/ppermute | solution.py:21
  212.5 17.2 %collective-permute-start = (f32[1,2,64,128]{3,2,0,1:T(8,128)S(1)}, f32[1,2,64,128]{3,2,0,1:T(8,128)S(1)}, u32[]{:S(2)}, u32[]{:S(2)}) collective-permute-start(f32[1,2,64,128]{3,2,0,1:T(8,128)S(1)} %get-tuple-element.298), channel_id=1, source_target_pairs={{0,16},{16,32},{32,48},{48,64},{64,80},{80,96},{96,112},{1,17},{17... | collective-permute-start | bytes 196616 | tf_op jit(solution)/shard_map/ppermute | solution.py:18
  227.1 5.6 collective-permute-start.1
  267.7 15.3 %collective-permute-start.4 = (f32[1,1,64,128]{3,2,0,1:T(8,128)S(1)}, f32[1,1,64,128]{3,2,0,1:T(8,128)S(1)}, u32[]{:S(2)}, u32[]{:S(2)}) collective-permute-start(f32[1,1,64,128]{3,2,0,1:T(8,128)S(1)} %get-tuple-element.325), channel_id=1, source_target_pairs={{0,16},{16,32},{32,48},{48,64},{64,80},{80,96},{96,112},{1,17},{17... | collective-permute-start | bytes 98312 | tf_op jit(solution)/shard_map/ppermute | solution.py:18
  281.0 5.2 collective-permute-start.5
  452.1 15.9 %collective-permute-start.6 = (f32[1,1,64,128]{3,2,0,1:T(8,128)S(1)}, f32[1,1,64,128]{3,2,0,1:T(8,128)S(1)}, u32[]{:S(2)}, u32[]{:S(2)}) collective-permute-start(f32[1,1,64,128]{3,2,0,1:T(8,128)S(1)} %get-tuple-element.321), channel_id=1, source_target_pairs={{0,16},{16,32},{32,48},{48,64},{64,80},{80,96},{96,112},{1,17},{17... | collective-permute-start | bytes 98312 | tf_op jit(solution)/shard_map/ppermute | solution.py:18
  466.0 5.2 collective-permute-start.7
  635.9 17.5 %collective-permute-start.8 = (f32[1,1,64,128]{3,2,0,1:T(8,128)S(1)}, f32[1,1,64,128]{3,2,0,1:T(8,128)S(1)}, u32[]{:S(2)}, u32[]{:S(2)}) collective-permute-start(f32[1,1,64,128]{3,2,0,1:T(8,128)S(1)} %get-tuple-element.317), channel_id=1, source_target_pairs={{0,16},{16,32},{32,48},{48,64},{64,80},{80,96},{96,112},{1,17},{17... | collective-permute-start | bytes 98312 | tf_op jit(solution)/shard_map/ppermute | solution.py:18
  651.5 5.2 collective-permute-start.9
  821.6 15.7 %collective-permute-start.10 = (f32[1,1,64,128]{3,2,0,1:T(8,128)S(1)}, f32[1,1,64,128]{3,2,0,1:T(8,128)S(1)}, u32[]{:S(2)}, u32[]{:S(2)}) collective-permute-start(f32[1,1,64,128]{3,2,0,1:T(8,128)S(1)} %get-tuple-element.313), channel_id=1, source_target_pairs={{0,16},{16,32},{32,48},{48,64},{64,80},{80,96},{96,112},{1,17},{17... | collective-permute-start | bytes 98312 | tf_op jit(solution)/shard_map/ppermute | solution.py:18
  834.7 5.2 collective-permute-start.11
  1005.6 17.4 %collective-permute-start.12 = (f32[1,1,64,128]{3,2,0,1:T(8,128)S(1)}, f32[1,1,64,128]{3,2,0,1:T(8,128)S(1)}, u32[]{:S(2)}, u32[]{:S(2)}) collective-permute-start(f32[1,1,64,128]{3,2,0,1:T(8,128)S(1)} %get-tuple-element.309), channel_id=1, source_target_pairs={{0,16},{16,32},{32,48},{48,64},{64,80},{80,96},{96,112},{1,17},{17... | collective-permute-start | bytes 98312 | tf_op jit(solution)/shard_map/ppermute | solution.py:18
  1021.0 5.2 collective-permute-start.13
  1191.3 15.7 %collective-permute-start.14 = (f32[1,1,64,128]{3,2,0,1:T(8,128)S(1)}, f32[1,1,64,128]{3,2,0,1:T(8,128)S(1)}, u32[]{:S(2)}, u32[]{:S(2)}) collective-permute-start(f32[1,1,64,128]{3,2,0,1:T(8,128)S(1)} %get-tuple-element.305), channel_id=1, source_target_pairs={{0,16},{16,32},{32,48},{48,64},{64,80},{80,96},{96,112},{1,17},{17... | collective-permute-start | bytes 98312 | tf_op jit(solution)/shard_map/ppermute | solution.py:18
  1204.3 5.2 collective-permute-start.15
Sparse Core Ops, SparseCore 0:
  15.3 46.3 all-gather.1
where the time goes:
time: 1340 us; the launch traced here: 1330 us
  blocking collectives  969 us (72%)
  other arithmetic  146 us (11%)
  starting transfers between devices  128 us (10%)
  local copies, waits for them, and re-layouts  29.9 us (2%)
  between operations  29.7 us (2%)
  waiting for transfers between devices  19.4 us (1%)
    psum x6, blocking collectives, weighted(): return lax.psum(jnp.sum(residual_now * precond_now), ('by', 'bx'))  381 us
    psum x5, blocking collectives, local(): lax.psum(jnp.sum(direction * image_field), ('by', 'bx'))  317 us
    all_gather x8, blocking collectives, extend(): lax.all_gather(edge_rows, 'bx', axis=1, tiled=True)  137 us
    all_gather x8, blocking collectives, extend(): lax.all_gather(edge_cols, 'bx', axis=1, tiled=True)  135 us
    ppermute x8, starting transfers between devices, padded_2(): lax.ppermute(lax.slice_in_dim(block, block.shape[dim] - width, None, axis...  111 us
    dynamic_update_slice x60, other arithmetic, column_step(): lax.scan(forward, start_carry, (-mixing_above, diagonal, -mixing, right_s...  101 us
  transfers between devices with their start and end apart: 17, of which 7 were waited for; matrix products, arithmetic and copies ran while one was open for 8% of the time, Pallas kernels for 0%

commit v1 on v0

--- a/solution.py
+++ b/solution.py
@@ -121,7 +121,9 @@
         edge_cols = jnp.stack([field_blocks[..., 0], field_blocks[..., -1]], axis=2)
         edge_rows = jnp.stack([field_blocks[..., 0, :], field_blocks[..., -1, :]], axis=2)
         gathered_cols, gathered_rows = (
-            lax.all_gather(edge_cols, "bx", axis=1, tiled=True),
+            jnp.concatenate(
+                lax.all_to_all(jnp.stack([edge_cols] * lax.axis_size("bx")), "bx", 0, 0), axis=1
+            ),
             lax.all_gather(edge_rows, "bx", axis=1, tiled=True),
         )
         geo_rows = jnp.einsum("ct,qtsw->sqcw", geo_pick, gathered_rows, precision=PRECISE)

time: 1340 us -> 1220 us (0.910)
  blocking collectives: 969 us -> 842 us
    all_gather x8 -> x0, blocking collectives: 135 us -> none  [extend(): lax.all_gather(edge_cols, 'bx', axis=1, tiled=True)]
    ppermute x8, starting transfers between devices: 111 us -> 75.2 us  [padded_2(): lax.ppermute(lax.slice_in_dim(block, block.shape[dim] - width, None, axis...]
    all_to_all x0 -> x8, starting transfers between devices: none -> 35.9 us  [extend(): lax.all_to_all(jnp.stack([edge_cols] * lax.axis_size('bx')), 'bx', 0, 0)]
  transfers between devices with their start and end apart: 17 -> 25, of which waited for: 7 -> 7; matrix products, arithmetic and copies ran while one was open for 8% -> 10% of each run, Pallas kernels for 0% -> 0%
where the time goes in v1:
time: 1220 us; the launch traced here: 1210 us
  blocking collectives  842 us (69%)
  other arithmetic  151 us (12%)
  starting transfers between devices  127 us (10%)
  local copies, waits for them, and re-layouts  37.3 us (3%)
  between operations  29.7 us (2%)
  waiting for transfers between devices  13.7 us (1%)
    psum x6, blocking collectives, weighted(): return lax.psum(jnp.sum(residual_now * precond_now), ('by', 'bx'))  378 us
    psum x5, blocking collectives, local(): lax.psum(jnp.sum(direction * image_field), ('by', 'bx'))  318 us
    all_gather x8, blocking collectives, extend(): lax.all_gather(edge_rows, 'bx', axis=1, tiled=True)  146 us
    dynamic_update_slice x60, other arithmetic, column_step(): lax.scan(forward, start_carry, (-mixing_above, diagonal, -mixing, right_s...  101 us
    ppermute x8, starting transfers between devices, padded_2(): lax.ppermute(lax.slice_in_dim(block, block.shape[dim] - width, None, axis...  75.2 us
    all_to_all x8, starting transfers between devices, extend(): lax.all_to_all(jnp.stack([edge_cols] * lax.axis_size('bx')), 'bx', 0, 0)  35.9 us
  transfers between devices with their start and end apart: 25, of which 7 were waited for; matrix products, arithmetic and copies ran while one was open for 10% of the time, Pallas kernels for 0%

profile of v1, /device:TPU:1, one launch (start us, length us, event | category | flops | bytes accessed | tf_op | source)
XLA Modules:
  0.0 1210.8 jit_solution(6045640837604264747)
XLA Ops:
  8.0 2.8 fusion.5
  10.9 2.7 pad_negate_fusion
  16.1 3.8 slice-done
  19.9 9.8 multiply_add_fusion.1
  29.7 9.2 slice.433
  38.9 15.5 %multiply_add_fusion = f32[20,4,16,2048]{3,2,1,0:T(8,128)} fusion(f32[19,4,16,2048]{3,2,1,0:T(8,128)} %slice.433, f32[20,4,16,2048]{3,2,1,0:T(8,128)} %param.14, f32[20,4,16,2048]{3,2,1,0:T(8,128)} %multiply_add_fusion.1, f32[4,16,2048]{2,1,0:T(8,128)S(1)} %fusion.3, f32[20,4,2048]{2,1,0:T(4,128)S(1)} %get-tuple-element.335, f32[20,4,2048]{2,1,0:T(4,128)S(1)} %fusion.2), kind=kLoop, calls=%fused_computation.13 | loop fusion | flops 13107200 | bytes 43253760 | tf_op jit(solution)/shard_map/add | solution.py:41
  54.4 5.3 broadcast.145.clone
  59.9 58.2 %while.34 = (s32[]{:T(128)}, f32[4,2048]{1,0:T(4,128)S(1)}, f32[4,16,2048]{2,1,0:T(8,128)S(1)}, f32[20,4,2048]{2,1,0:T(4,128)S(1)}, f32[20,4,16,2048]{3,2,1,0:T(...) while((s32[]{:T(128)}, f32[4,2048]{1,0:T(4,128)S(1)}, ...), condition=%wide.region_1.2_spmd.clone, body=%wide.region_0.0_spmd.clone.sunk | while | flops 557059 | bytes 2425468 | solution.py:55
  119.7 3.0 convolution_bitcast_fusion
  123.8 7.7 all-to-all-start.1
  131.5 18.3 %all_gather.29 = f32[1,64,2,128]{3,2,0,1:T(2,128)S(1)} all-gather(f32[1,4,2,128]{3,2,0,1:T(2,128)S(1)} %maximum_bitcast_fusion.7), channel_id=1, replica_groups=mesh['by'=8,'bx'=16] {'bx'}, dimensions={1}, use_global_device_ids=true | all-gather | bytes 69632 | tf_op jit(solution)/shard_map/all_gather | solution.py:127
  150.1 9.8 collective-permute-start.2
  162.0 17.5 %all_gather.28 = f32[2,64,2,128]{3,2,0,1:T(2,128)S(1)} all-gather(f32[2,4,2,128]{3,2,0,1:T(2,128)S(1)} %fusion.128), channel_id=1, replica_groups=mesh['by'=8,'bx'=16] {'bx'}, dimensions={1}, use_global_device_ids=true | all-gather | bytes 139264 | tf_op jit(solution)/shard_map/all_gather | solution.py:127
  180.6 9.1 collective-permute-start
  191.6 3.8 all-to-all-start
  197.4 4.5 all-to-all-done
  206.0 3.5 all-to-all-start.2
  209.5 18.5 %all_gather.30 = f32[1,64,2,128]{3,2,0,1:T(2,128)S(1)} all-gather(f32[1,4,2,128]{3,2,0,1:T(2,128)S(1)} %maximum_bitcast_fusion.8), channel_id=1, replica_groups=mesh['by'=8,'bx'=16] {'bx'}, dimensions={1}, use_global_device_ids=true | all-gather | bytes 69632 | tf_op jit(solution)/shard_map/all_gather | solution.py:127
  228.1 10.8 collective-permute-start.4
  245.3 64.4 %all-reduce.19 = (f32[]{:T(128)}, f32[]{:T(128)}) all-reduce(f32[]{:T(128)} %get-tuple-element.219, f32[]{:T(128)} %get-tuple-element.218), channel_id=1, replica_groups=mesh['by'=8,'bx'=16] {'by','bx'}, use_global_device_ids=true, to_apply=%region_6.7 | all-reduce | flops 2 | bytes 16 | tf_op jit(solution)/shard_map/psum | solution.py:168
  311.7 62.9 %psum.86 = f32[]{:T(128)} all-reduce(f32[]{:T(128)} %get-tuple-element.278), channel_id=1, replica_groups=mesh['by'=8,'bx'=16] {'by','bx'}, use_global_device_ids=true, to_apply=%region_10.11 | all-reduce | flops 1 | bytes 8 | tf_op jit(solution)/shard_map/psum | solution.py:168
  376.8 3.9 all-to-all-start.3
  380.7 18.3 %all_gather.31 = f32[1,64,2,128]{3,2,0,1:T(2,128)S(1)} all-gather(f32[1,4,2,128]{3,2,0,1:T(2,128)S(1)} %maximum_bitcast_fusion.9), channel_id=1, replica_groups=mesh['by'=8,'bx'=16] {'bx'}, dimensions={1}, use_global_device_ids=true | all-gather | bytes 69632 | tf_op jit(solution)/shard_map/all_gather | solution.py:127
  399.3 8.9 collective-permute-start.6
  414.5 63.7 %psum.87 = f32[]{:T(128)} all-reduce(f32[]{:T(128)} %get-tuple-element.276), channel_id=1, replica_groups=mesh['by'=8,'bx'=16] {'by','bx'}, use_global_device_ids=true, to_apply=%region_12.13 | all-reduce | flops 1 | bytes 8 | tf_op jit(solution)/shard_map/psum | solution.py:174
  480.0 62.6 %psum.88 = f32[]{:T(128)} all-reduce(f32[]{:T(128)} %get-tuple-element.273), channel_id=1, replica_groups=mesh['by'=8,'bx'=16] {'by','bx'}, use_global_device_ids=true, to_apply=%region_14.15 | all-reduce | flops 1 | bytes 8 | tf_op jit(solution)/shard_map/psum | solution.py:168
  544.8 4.3 all-to-all-start.4
  549.1 18.3 %all_gather.32 = f32[1,64,2,128]{3,2,0,1:T(2,128)S(1)} all-gather(f32[1,4,2,128]{3,2,0,1:T(2,128)S(1)} %maximum_bitcast_fusion.10), channel_id=1, replica_groups=mesh['by'=8,'bx'=16] {'bx'}, dimensions={1}, use_global_device_ids=true | all-gather | bytes 69632 | tf_op jit(solution)/shard_map/all_gather | solution.py:127
  567.7 8.9 collective-permute-start.8
  582.9 63.7 %psum.89 = f32[]{:T(128)} all-reduce(f32[]{:T(128)} %get-tuple-element.271), channel_id=1, replica_groups=mesh['by'=8,'bx'=16] {'by','bx'}, use_global_device_ids=true, to_apply=%region_16.17 | all-reduce | flops 1 | bytes 8 | tf_op jit(solution)/shard_map/psum | solution.py:174
  648.6 62.6 %psum.90 = f32[]{:T(128)} all-reduce(f32[]{:T(128)} %get-tuple-element.268), channel_id=1, replica_groups=mesh['by'=8,'bx'=16] {'by','bx'}, use_global_device_ids=true, to_apply=%region_18.19 | all-reduce | flops 1 | bytes 8 | tf_op jit(solution)/shard_map/psum | solution.py:168
  713.4 4.3 all-to-all-start.5
  717.7 18.3 %all_gather.33 = f32[1,64,2,128]{3,2,0,1:T(2,128)S(1)} all-gather(f32[1,4,2,128]{3,2,0,1:T(2,128)S(1)} %maximum_bitcast_fusion.11), channel_id=1, replica_groups=mesh['by'=8,'bx'=16] {'bx'}, dimensions={1}, use_global_device_ids=true | all-gather | bytes 69632 | tf_op jit(solution)/shard_map/all_gather | solution.py:127
  736.3 9.2 collective-permute-start.10
  751.8 63.7 %psum.91 = f32[]{:T(128)} all-reduce(f32[]{:T(128)} %get-tuple-element.266), channel_id=1, replica_groups=mesh['by'=8,'bx'=16] {'by','bx'}, use_global_device_ids=true, to_apply=%region_20.21 | all-reduce | flops 1 | bytes 8 | tf_op jit(solution)/shard_map/psum | solution.py:174
  817.3 62.7 %psum.92 = f32[]{:T(128)} all-reduce(f32[]{:T(128)} %get-tuple-element.263), channel_id=1, replica_groups=mesh['by'=8,'bx'=16] {'by','bx'}, use_global_device_ids=true, to_apply=%region_22.23 | all-reduce | flops 1 | bytes 8 | tf_op jit(solution)/shard_map/psum | solution.py:168
  882.2 4.2 all-to-all-start.6
  886.5 18.3 %all_gather.34 = f32[1,64,2,128]{3,2,0,1:T(2,128)S(1)} all-gather(f32[1,4,2,128]{3,2,0,1:T(2,128)S(1)} %maximum_bitcast_fusion.12), channel_id=1, replica_groups=mesh['by'=8,'bx'=16] {'bx'}, dimensions={1}, use_global_device_ids=true | all-gather | bytes 69632 | tf_op jit(solution)/shard_map/all_gather | solution.py:127
  905.0 9.2 collective-permute-start.12
  920.5 63.7 %psum.93 = f32[]{:T(128)} all-reduce(f32[]{:T(128)} %get-tuple-element.261), channel_id=1, replica_groups=mesh['by'=8,'bx'=16] {'by','bx'}, use_global_device_ids=true, to_apply=%region_24.25 | all-reduce | flops 1 | bytes 8 | tf_op jit(solution)/shard_map/psum | solution.py:174
  986.2 62.7 %psum.94 = f32[]{:T(128)} all-reduce(f32[]{:T(128)} %multiply_reduce_fusion), channel_id=1, replica_groups=mesh['by'=8,'bx'=16] {'by','bx'}, use_global_device_ids=true, to_apply=%region_26.27 | all-reduce | flops 1 | bytes 8 | tf_op jit(solution)/shard_map/psum | solution.py:168
  1051.2 4.2 all-to-all-start.7
  1055.5 18.3 %all_gather.35 = f32[1,64,2,128]{3,2,0,1:T(2,128)S(1)} all-gather(f32[1,4,2,128]{3,2,0,1:T(2,128)S(1)} %maximum_bitcast_fusion.13), channel_id=1, replica_groups=mesh['by'=8,'bx'=16] {'bx'}, dimensions={1}, use_global_device_ids=true | all-gather | bytes 69632 | tf_op jit(solution)/shard_map/all_gather | solution.py:127
  1074.0 9.2 collective-permute-start.14
  1089.5 5.4 broadcast.145
  1094.9 43.3 %while.35 = (s32[]{:T(128)}, f32[4,16,2048]{2,1,0:T(8,128)S(1)}, f32[20,4,16,2048]{3,2,1,0:T(8,128)}, f32[20,4,16,2048]{3,2,1,0:T(8,128)}, f32[20,4,2048]{2,1,0:T(4,128)S(1)}, /*index=5*/s32[]{:T(128)}, s32[]{:T(128)}, s32[]{:T(128)}) while((s32[]{:T(128)}, f32[4,16,2048]{2,1,0:T(8,128)S(1)}, f32[20,4,16,2048]{3,2,1,0:T(8,128)}, ...), condition=%wide.region_3.4_spmd.clone, body=%wide.region_2.3_spmd.clone.sunk | while | flops 393220 | bytes 2195571 | solution.py:64
  1095.0 2.2 bitcast_dynamic-update-slice_fusion.8
  1138.3 63.7 %psum.95 = f32[]{:T(128)} all-reduce(f32[]{:T(128)} %fusion.39), channel_id=1, replica_groups=mesh['by'=8,'bx'=16] {'by','bx'}, use_global_device_ids=true, to_apply=%region_28.29 | all-reduce | flops 1 | bytes 8 | tf_op jit(solution)/shard_map/psum | solution.py:174
  (344 shorter events, 163.8 us)
Async XLA Ops:
  7.2 112.6 %all-gather.2.cloned.1.call-start = ((), (), s32[]{:S(2)}) async-start(), calls=%async_computation.8 | async-start | bytes 2228224 | tf_op jit(solution)/shard_map/all_gather | solution.py:105
  16.1 3.8 slice-start
  29.7 9.2 copy-start.1
  54.4 65.2 %copy-start = (s32[4,16,128]{2,1,0:T(8,128)S(1)}, s32[4,16,128]{2,1,0:T(8,128)}, u32[]{:S(2)}) copy-start(s32[4,16,128]{2,1,0:T(8,128)} %param.21) | copy-start | bytes 98308
  123.8 67.8 %all-to-all-start.1 = ((f32[16,1,128]{2,1,0:T(1,128)}), f32[16,1,128]{2,1,0:T(1,128)S(1)}, u32[]{:S(2)}, u32[]{:S(2)}) async-start(f32[16,1,128]{2,1,0:T(1,128)} %reshape.329), calls=%async_computation.1 | async-start | bytes 16384 | tf_op jit(solution)/shard_map/all_to_all | solution.py:125
  150.1 53.3 %collective-permute-start.2 = (f32[1,1,64,128]{3,2,0,1:T(8,128)S(1)}, f32[1,1,64,128]{3,2,0,1:T(8,128)S(1)}, u32[]{:S(2)}, u32[]{:S(2)}) collective-permute-start(f32[1,1,64,128]{3,2,0,1:T(8,128)S(1)} %get-tuple-element.331), channel_id=1, source_target_pairs={{0,16},{16,32},{32,48},{48,64},{64,80},{80,96},{96,112},{1,17},{17... | collective-permute-start | bytes 98312 | tf_op jit(solution)/shard_map/ppermute | solution.py:18
  159.8 43.9 %collective-permute-start.3 = (f32[1,1,64,128]{3,2,0,1:T(8,128)S(1)}, f32[1,1,64,128]{3,2,0,1:T(8,128)S(1)}, u32[]{:S(2)}, u32[]{:S(2)}) collective-permute-start(f32[1,1,64,128]{3,2,0,1:T(8,128)S(1)} %get-tuple-element.332), channel_id=1, source_target_pairs={{16,0},{32,16},{48,32},{64,48},{80,64},{96,80},{112,96},{17,1},{33... | collective-permute-start | bytes 98312 | tf_op jit(solution)/shard_map/ppermute | solution.py:21
  180.6 23.5 %collective-permute-start = (f32[1,2,64,128]{3,2,0,1:T(8,128)S(1)}, f32[1,2,64,128]{3,2,0,1:T(8,128)S(1)}, u32[]{:S(2)}, u32[]{:S(2)}) collective-permute-start(f32[1,2,64,128]{3,2,0,1:T(8,128)S(1)} %get-tuple-element.300), channel_id=1, source_target_pairs={{0,16},{16,32},{32,48},{48,64},{64,80},{80,96},{96,112},{1,17},{17... | collective-permute-start | bytes 196616 | tf_op jit(solution)/shard_map/ppermute | solution.py:18
  189.7 14.7 %collective-permute-start.1 = (f32[1,2,64,128]{3,2,0,1:T(8,128)S(1)}, f32[1,2,64,128]{3,2,0,1:T(8,128)S(1)}, u32[]{:S(2)}, u32[]{:S(2)}) collective-permute-start(f32[1,2,64,128]{3,2,0,1:T(8,128)S(1)} %get-tuple-element.301), channel_id=1, source_target_pairs={{16,0},{32,16},{48,32},{64,48},{80,64},{96,80},{112,96},{17,1},{33... | collective-permute-start | bytes 196616 | tf_op jit(solution)/shard_map/ppermute | solution.py:21
  191.6 10.2 all-to-all-start
  206.0 34.9 %all-to-all-start.2 = ((f32[16,1,128]{2,1,0:T(1,128)}), f32[16,1,128]{2,1,0:T(1,128)S(1)}, u32[]{:S(2)}, u32[]{:S(2)}) async-start(f32[16,1,128]{2,1,0:T(1,128)} %reshape.331), calls=%async_computation.2 | async-start | bytes 16384 | tf_op jit(solution)/shard_map/all_to_all | solution.py:125
  228.1 14.3 %collective-permute-start.4 = (f32[1,1,64,128]{3,2,0,1:T(8,128)S(1)}, f32[1,1,64,128]{3,2,0,1:T(8,128)S(1)}, u32[]{:S(2)}, u32[]{:S(2)}) collective-permute-start(f32[1,1,64,128]{3,2,0,1:T(8,128)S(1)} %get-tuple-element.325), channel_id=1, source_target_pairs={{0,16},{16,32},{32,48},{48,64},{64,80},{80,96},{96,112},{1,17},{17... | collective-permute-start | bytes 98312 | tf_op jit(solution)/shard_map/ppermute | solution.py:18
  239.0 5.2 collective-permute-start.5
  376.8 33.3 %all-to-all-start.3 = ((f32[16,1,128]{2,1,0:T(1,128)}), f32[16,1,128]{2,1,0:T(1,128)S(1)}, u32[]{:S(2)}, u32[]{:S(2)}) async-start(f32[16,1,128]{2,1,0:T(1,128)} %reshape.333), calls=%async_computation.3 | async-start | bytes 16384 | tf_op jit(solution)/shard_map/all_to_all | solution.py:125
  399.3 12.3 %collective-permute-start.6 = (f32[1,1,64,128]{3,2,0,1:T(8,128)S(1)}, f32[1,1,64,128]{3,2,0,1:T(8,128)S(1)}, u32[]{:S(2)}, u32[]{:S(2)}) collective-permute-start(f32[1,1,64,128]{3,2,0,1:T(8,128)S(1)} %get-tuple-element.321), channel_id=1, source_target_pairs={{0,16},{16,32},{32,48},{48,64},{64,80},{80,96},{96,112},{1,17},{17... | collective-permute-start | bytes 98312 | tf_op jit(solution)/shard_map/ppermute | solution.py:18
  408.1 5.2 collective-permute-start.7
  544.8 33.8 %all-to-all-start.4 = ((f32[16,1,128]{2,1,0:T(1,128)}), f32[16,1,128]{2,1,0:T(1,128)S(1)}, u32[]{:S(2)}, u32[]{:S(2)}) async-start(f32[16,1,128]{2,1,0:T(1,128)} %reshape.335), calls=%async_computation.4 | async-start | bytes 16384 | tf_op jit(solution)/shard_map/all_to_all | solution.py:125
  567.7 12.3 %collective-permute-start.8 = (f32[1,1,64,128]{3,2,0,1:T(8,128)S(1)}, f32[1,1,64,128]{3,2,0,1:T(8,128)S(1)}, u32[]{:S(2)}, u32[]{:S(2)}) collective-permute-start(f32[1,1,64,128]{3,2,0,1:T(8,128)S(1)} %get-tuple-element.317), channel_id=1, source_target_pairs={{0,16},{16,32},{32,48},{48,64},{64,80},{80,96},{96,112},{1,17},{17... | collective-permute-start | bytes 98312 | tf_op jit(solution)/shard_map/ppermute | solution.py:18
  576.6 5.2 collective-permute-start.9
  713.4 34.3 %all-to-all-start.5 = ((f32[16,1,128]{2,1,0:T(1,128)}), f32[16,1,128]{2,1,0:T(1,128)S(1)}, u32[]{:S(2)}, u32[]{:S(2)}) async-start(f32[16,1,128]{2,1,0:T(1,128)} %reshape.337), calls=%async_computation.5 | async-start | bytes 16384 | tf_op jit(solution)/shard_map/all_to_all | solution.py:125
  736.3 12.8 %collective-permute-start.10 = (f32[1,1,64,128]{3,2,0,1:T(8,128)S(1)}, f32[1,1,64,128]{3,2,0,1:T(8,128)S(1)}, u32[]{:S(2)}, u32[]{:S(2)}) collective-permute-start(f32[1,1,64,128]{3,2,0,1:T(8,128)S(1)} %get-tuple-element.313), channel_id=1, source_target_pairs={{0,16},{16,32},{32,48},{48,64},{64,80},{80,96},{96,112},{1,17},{17... | collective-permute-start | bytes 98312 | tf_op jit(solution)/shard_map/ppermute | solution.py:18
  745.5 5.2 collective-permute-start.11
  882.2 33.9 %all-to-all-start.6 = ((f32[16,1,128]{2,1,0:T(1,128)}), f32[16,1,128]{2,1,0:T(1,128)S(1)}, u32[]{:S(2)}, u32[]{:S(2)}) async-start(f32[16,1,128]{2,1,0:T(1,128)} %reshape.339), calls=%async_computation.6 | async-start | bytes 16384 | tf_op jit(solution)/shard_map/all_to_all | solution.py:125
  905.0 12.6 %collective-permute-start.12 = (f32[1,1,64,128]{3,2,0,1:T(8,128)S(1)}, f32[1,1,64,128]{3,2,0,1:T(8,128)S(1)}, u32[]{:S(2)}, u32[]{:S(2)}) collective-permute-start(f32[1,1,64,128]{3,2,0,1:T(8,128)S(1)} %get-tuple-element.309), channel_id=1, source_target_pairs={{0,16},{16,32},{32,48},{48,64},{64,80},{80,96},{96,112},{1,17},{17... | collective-permute-start | bytes 98312 | tf_op jit(solution)/shard_map/ppermute | solution.py:18
  914.2 5.2 collective-permute-start.13
  1051.2 33.9 %all-to-all-start.7 = ((f32[16,1,128]{2,1,0:T(1,128)}), f32[16,1,128]{2,1,0:T(1,128)S(1)}, u32[]{:S(2)}, u32[]{:S(2)}) async-start(f32[16,1,128]{2,1,0:T(1,128)} %reshape.341), calls=%async_computation.7 | async-start | bytes 16384 | tf_op jit(solution)/shard_map/all_to_all | solution.py:125
  1074.0 12.6 %collective-permute-start.14 = (f32[1,1,64,128]{3,2,0,1:T(8,128)S(1)}, f32[1,1,64,128]{3,2,0,1:T(8,128)S(1)}, u32[]{:S(2)}, u32[]{:S(2)}) collective-permute-start(f32[1,1,64,128]{3,2,0,1:T(8,128)S(1)} %get-tuple-element.305), channel_id=1, source_target_pairs={{0,16},{16,32},{32,48},{48,64},{64,80},{80,96},{96,112},{1,17},{17... | collective-permute-start | bytes 98312 | tf_op jit(solution)/shard_map/ppermute | solution.py:18
  1083.2 5.2 collective-permute-start.15
Sparse Core Ops, SparseCore 0:
  15.3 46.3 all-gather.1
